TPU v7x, 32 devices: a whole 2x2x4 slice. The times are simulated.
32 devices in a mesh: gx: 4 (over z), gy: 8 (over y, x, core).
Axes of the slice: x: 2, y: 2, z: 4, core: 2. Of those that a mesh axis runs over, the one named last changes fastest.
Arguments:
- forcing: float32 [16, 128, 512], P(None, 'gy', 'gx'), may hold values from -6 to 6
- pressure_in: float32 [16, 128, 512], P(None, 'gy', 'gx'), may hold values from -6 to 6
- x_coupling: float32 [16, 128, 512], P(None, 'gy', 'gx'), may hold values from 0.5 to 2000
- y_coupling: float32 [16, 128, 512], P(None, 'gy', 'gx'), may hold values from 0.5 to 2000
- z_coupling: float32 [16, 128, 512], P(None, 'gy', 'gx'), may hold values from 0.05 to 0.5
- damping: float32 [16, 128, 512], P(None, 'gy', 'gx'), may hold values from 0.2 to 2
Outputs:
- pressure: float32 [16, 128, 512], P(None, 'gy', 'gx')
- coarse_residual: float32 [8, 64, 256], P(None, 'gy', 'gx')
- coarse_correction: float32 [8, 64, 256], P(None, 'gy')
All inputs are finite; a program needn't handle non-finite values.
Results may differ from a plain program's by a relative error of at most 0.0001.
Values sent between devices are 32-bit elements; how exact they have to be, the bound alone decides.
A program may use at most 128 MiB of HBM per device.

v0:
```python
import jax
import jax.numpy as jnp
from jax import lax
from jax.sharding import PartitionSpec as P

COARSE = 3
RELAX = 0.8


def extended(value, sides, width):
    for axis, dim in sides:
        peers, length = (lax.axis_size(axis), value.shape[dim])
        up = [(i, (i + 1) % peers) for i in range(peers - 1)]
        down = [(j, i) for i, j in up]
        last = lax.slice_in_dim(value, length - width, length, axis=dim)
        leading = lax.slice_in_dim(value, 0, width, axis=dim)
        before = lax.ppermute(last, axis, up)
        after = lax.ppermute(leading, axis, down)
        value = jnp.concatenate([before, value, after], axis=dim)
    return value


def from_behind(value, axis, steps):
    count = lax.axis_size(axis)
    leading, last = (max(0, -steps), min(count, count - steps))
    return lax.ppermute(value, axis, [(source, source + steps) for source in range(leading, last)])


def shifted(values, offset, axis_dim, filler):
    length = values.shape[axis_dim]
    if offset > 0:
        border = jnp.full_like(lax.slice_in_dim(values, 0, offset, axis=axis_dim), filler)
        return jnp.concatenate(
            [border, lax.slice_in_dim(values, 0, length - offset, axis=axis_dim)], axis=axis_dim
        )
    amount = -offset
    border = jnp.full_like(lax.slice_in_dim(values, 0, amount, axis=axis_dim), filler)
    return jnp.concatenate(
        [lax.slice_in_dim(values, amount, length, axis=axis_dim), border], axis=axis_dim
    )


def line_solve(low_band, diagonal, up_band, right_side, axis_dim):
    length = right_side.shape[axis_dim]
    stride = 1
    while stride < length:
        before = shifted(diagonal, stride, axis_dim, 1.0)
        after = shifted(diagonal, -stride, axis_dim, 1.0)
        weight_low = -low_band / before
        weight_up = -up_band / after
        new_diag = (
            diagonal
            + weight_low * shifted(up_band, stride, axis_dim, 0.0)
            + weight_up * shifted(low_band, -stride, axis_dim, 0.0)
        )
        new_right = (
            right_side
            + weight_low * shifted(right_side, stride, axis_dim, 0.0)
            + weight_up * shifted(right_side, -stride, axis_dim, 0.0)
        )
        low_band = weight_low * shifted(low_band, stride, axis_dim, 0.0)
        up_band = weight_up * shifted(up_band, -stride, axis_dim, 0.0)
        diagonal = new_diag
        right_side = new_right
        stride = stride * 2
    return right_side / diagonal


def top_masked(coupling):
    levels = coupling.shape[0]
    keep = (jnp.arange(levels) < levels - 1)[:, None, None]
    return jnp.where(keep, coupling, jnp.zeros_like(coupling))


def vertical(field, z_low, z_top):
    return z_low * shifted(field, 1, 0, 0.0) + z_top * shifted(field, -1, 0, 0.0)


def restrict(field):
    levels, rows, columns = field.shape
    blocks = field.reshape(levels // 2, 2, rows // 2, 2, columns // 2, 2)
    return jnp.sum(blocks, axis=(1, 3, 5)) * 0.125


def y_rim(field):
    return extended(field, (("gy", 1),), 1)


def x_return(solved):
    return lax.all_to_all(solved, "gx", split_axis=2, concat_axis=0, tiled=True)


def y_return(solved):
    return lax.all_to_all(solved, "gy", split_axis=1, concat_axis=0, tiled=True)


def x_solve(diag_lines, band_lines, source_lines):
    return line_solve(-shifted(band_lines, 1, 2, 0.0), diag_lines, -band_lines, source_lines, 2)


def y_solve(diag_lines, band_lines, source_lines):
    return line_solve(-shifted(band_lines, 1, 1, 0.0), diag_lines, -band_lines, source_lines, 1)


def body(forcing, pressure_in, x_coupling, y_coupling, z_coupling, damping):
    z_top = top_masked(z_coupling)
    z_low = shifted(z_top, 1, 0, 0.0)
    x_left = jnp.concatenate(
        [from_behind(x_coupling[:, :, -1:], "gx", 1), x_coupling[:, :, :-1]], axis=2
    )
    y_left = jnp.concatenate(
        [from_behind(y_coupling[:, -1:, :], "gy", 1), y_coupling[:, :-1, :]], axis=1
    )
    diagonal = x_left + x_coupling + y_left + y_coupling + z_low + z_top + damping
    field = pressure_in
    for repeat in range(2):
        padded = y_rim(field)
        source = (
            forcing
            + y_left * padded[:, :-2, :]
            + y_coupling * padded[:, 2:, :]
            + vertical(field, z_low, z_top)
        )
        source_lines, diag_lines, band_lines = (
            lax.all_to_all(source, "gx", split_axis=0, concat_axis=2, tiled=True),
            lax.all_to_all(diagonal, "gx", split_axis=0, concat_axis=2, tiled=True),
            lax.all_to_all(x_coupling, "gx", split_axis=0, concat_axis=2, tiled=True),
        )
        field = x_return(x_solve(diag_lines, band_lines, source_lines))
        padded = extended(field, (("gx", 2),), 1)
        source = (
            forcing
            + x_left * padded[:, :, :-2]
            + x_coupling * padded[:, :, 2:]
            + vertical(field, z_low, z_top)
        )
        source_lines, diag_lines, band_lines = (
            lax.all_to_all(source, "gy", split_axis=0, concat_axis=1, tiled=True),
            lax.all_to_all(diagonal, "gy", split_axis=0, concat_axis=1, tiled=True),
            lax.all_to_all(y_coupling, "gy", split_axis=0, concat_axis=1, tiled=True),
        )
        field = y_return(y_solve(diag_lines, band_lines, source_lines))
    padded = extended(field, (("gy", 1), ("gx", 2)), 1)
    applied = (
        diagonal * field
        - x_left * padded[:, 1:-1, :-2]
        - x_coupling * padded[:, 1:-1, 2:]
        - y_left * padded[:, :-2, 1:-1]
        - y_coupling * padded[:, 2:, 1:-1]
        - vertical(field, z_low, z_top)
    )
    coarse_residual = restrict(forcing - applied)
    coarse_x = restrict(x_coupling)
    coarse_y = restrict(y_coupling)
    coarse_z = restrict(z_coupling)
    coarse_damp = restrict(damping)
    whole_res, whole_x, whole_y, whole_z, whole_damp = (
        lax.all_gather(coarse_residual, "gx", axis=2, tiled=True),
        lax.all_gather(coarse_x, "gx", axis=2, tiled=True),
        lax.all_gather(coarse_y, "gx", axis=2, tiled=True),
        lax.all_gather(coarse_z, "gx", axis=2, tiled=True),
        lax.all_gather(coarse_damp, "gx", axis=2, tiled=True),
    )
    cz_top = top_masked(whole_z)
    cz_low = shifted(cz_top, 1, 0, 0.0)
    cx_left = shifted(whole_x, 1, 2, 0.0)
    cy_left = jnp.concatenate(
        [from_behind(whole_y[:, -1:, :], "gy", 1), whole_y[:, :-1, :]], axis=1
    )
    coarse_diag = cx_left + whole_x + cy_left + whole_y + cz_low + cz_top + whole_damp
    correction = RELAX * whole_res / coarse_diag
    for repeat in range(COARSE - 1):
        padded = extended(correction, (("gy", 1),), 1)
        applied_coarse = (
            coarse_diag * correction
            - cx_left * shifted(correction, 1, 2, 0.0)
            - whole_x * shifted(correction, -1, 2, 0.0)
            - cy_left * padded[:, :-2, :]
            - whole_y * padded[:, 2:, :]
            - vertical(correction, cz_low, cz_top)
        )
        correction = correction + RELAX * (whole_res - applied_coarse) / coarse_diag
    return (field, coarse_residual, correction)


def solution(mesh):
    in_specs = (
        P(None, "gy", "gx"),
        P(None, "gy", "gx"),
        P(None, "gy", "gx"),
        P(None, "gy", "gx"),
        P(None, "gy", "gx"),
        P(None, "gy", "gx"),
    )
    out_specs = (P(None, "gy", "gx"), P(None, "gy", "gx"), P(None, "gy", None))
    return jax.shard_map(body, mesh=mesh, in_specs=in_specs, out_specs=out_specs, check_vma=False)
```

profile of v0, /device:TPU:4, one launch (start us, length us, event | category | flops | bytes accessed | tf_op | source)
XLA Modules:
  0.0 384.3 jit_solution(15006799556907630283)
XLA Ops:
  0.6 4.9 %all-to-all-start.1 = ((f32[16,16,128]{2,1,0:T(8,128)}), f32[16,16,128]{2,1,0:T(8,128)S(1)}, u32[]{:S(2)}, u32[]{:S(2)}) async-start(f32[16,16,128]{2,1,0:T(8,128)} %param.8), calls=%async_computation.1 | async-start | bytes 262144 | tf_op jit(solution)/shard_map/all_to_all | solution.py:127
  8.3 4.5 %collective-permute-start.3 = (f32[16,1,128]{2,1,0:T(1,128)S(1)}, f32[16,1,128]{2,1,0:T(1,128)S(1)}, u32[]{:S(2)}, u32[]{:S(2)}) collective-permute-start(f32[16,1,128]{2,1,0:T(1,128)S(1)} %get-tuple-element.266), channel_id=1, source_target_pairs={{1,0},{2,1},{3,2},{4,3},{5,4},{6,5},{7,6},{9,8},{10,9},{11,10},{12... | collective-permute-start | bytes 24584 | tf_op jit(solution)/shard_map/ppermute | solution.py:18
  16.6 3.9 %collective-permute-start = (f32[16,16,1]{2,1,0:T(8,128)S(1)}, f32[16,16,1]{2,1,0:T(8,128)S(1)}, u32[]{:S(2)}, u32[]{:S(2)}) collective-permute-start(f32[16,16,1]{2,1,0:T(8,128)S(1)} %slice.761), channel_id=1, source_target_pairs={{0,8},{8,16},{16,24},{1,9},{9,17},{17,25},{2,10},{10,18},{18,26},{... | collective-permute-start | bytes 3080 | tf_op jit(solution)/shard_map/ppermute | solution.py:26
  26.4 11.4 %all_to_all.236 = f32[16,16,128]{2,1,0:T(8,128)S(1)} all-to-all(f32[16,16,128]{2,1,0:T(8,128)S(1)} %get-tuple-element.78), channel_id=1, replica_groups=mesh['gx'=4,'gy'=8] {'gx'}, dimensions={0} | all-to-all | bytes 262144 | tf_op jit(solution)/shard_map/all_to_all | solution.py:125
  41.4 5.6 %all-to-all-done.2 = f32[16,16,128]{2,1,0:T(8,128)S(1)} async-done(((f32[16,16,128]{2,1,0:T(8,128)}), f32[16,16,128]{2,1,0:T(8,128)S(1)}, u32[]{:S(2)}, u32[]{:S(2)}) %all-to-all-start.2) | async-done | bytes 131104 | tf_op jit(solution)/shard_map/all_to_all | solution.py:126
  56.7 4.2 %all-to-all-start.6 = ((f32[16,16,128]{2,1,0:T(8,128)}), f32[16,16,128]{2,1,0:T(8,128)S(1)}, u32[]{:S(2)}, u32[]{:S(2)}) async-start(f32[16,16,128]{2,1,0:T(8,128)} %get-tuple-element.76), calls=%async_computation.6 | async-start | bytes 262144 | tf_op jit(solution)/shard_map/all_to_all | solution.py:139
  68.3 9.7 %reshape.31 = f32[8,2,8,2,64,2]{5,4,3,2,1,0:T(8,128)} reshape(f32[16,16,128]{2,1,0:T(8,128)S(1)} %copy-done) | data formatting | bytes 262144 | tf_op jit(solution)/shard_map/reshape | solution.py:81
  78.0 4.7 %reduce_sum.47 = f32[8,8,64]{2,1,0:T(8,128)} reduce(f32[8,2,8,2,64,2]{5,4,3,2,1,0:T(8,128)} %reshape.31, f32[]{:T(128)} %constant.7.clone.1), dimensions={1,3,5}, to_apply=%region_2.3 | reduce | flops 28672 | bytes 147460 | tf_op jit(solution)/shard_map/reduce_sum | solution.py:82
  91.7 4.4 %collective-permute-done.5 = f32[16,16,1]{2,1,0:T(8,128)S(1)} collective-permute-done((f32[16,16,1]{2,1,0:T(8,128)S(1)}, f32[16,16,1]{2,1,0:T(8,128)S(1)}, u32[]{:S(2)}, u32[]{:S(2)}) %collective-permute-start.5) | collective-permute-done | bytes 1056 | tf_op jit(solution)/shard_map/ppermute | solution.py:18
  97.0 4.8 %all-to-all-start.4 = ((f32[16,16,128]{2,1,0:T(8,128)}), f32[16,16,128]{2,1,0:T(8,128)S(1)}, u32[]{:S(2)}, u32[]{:S(2)}) async-start(f32[16,16,128]{2,1,0:T(8,128)} %fusion.22), calls=%async_computation.4 | async-start | bytes 262144 | tf_op jit(solution)/shard_map/all_to_all | solution.py:138
  101.8 4.0 %all-to-all-done.4 = f32[16,16,128]{2,1,0:T(8,128)S(1)} async-done(((f32[16,16,128]{2,1,0:T(8,128)}), f32[16,16,128]{2,1,0:T(8,128)S(1)}, u32[]{:S(2)}, u32[]{:S(2)}) %all-to-all-start.4) | async-done | bytes 131104 | tf_op jit(solution)/shard_map/all_to_all | solution.py:138
  109.7 5.6 %all-to-all-start.7 = ((f32[2,128,128]{2,0,1:T(2,128)}), f32[2,128,128]{2,0,1:T(2,128)}, u32[]{:S(2)}, u32[]{:S(2)}) async-start(f32[2,128,128]{2,0,1:T(2,128)} %copy.192), calls=%async_computation.7 | async-start | bytes 262144 | tf_op jit(solution)/shard_map/all_to_all | solution.py:94
  115.5 21.7 %all_gather.17 = f32[8,8,256]{1,0,2:T(8,128)S(1)} all-gather(f32[8,8,64]{1,0,2:T(8,128)S(1)} %copy.208), channel_id=1, replica_groups=mesh['gx'=4,'gy'=8] {'gx'}, dimensions={2}, use_global_device_ids=true | all-gather | bytes 81920 | tf_op jit(solution)/shard_map/all_gather | solution.py:160
  139.9 9.7 %reshape.32 = f32[8,2,8,2,64,2]{5,4,3,2,1,0:T(8,128)} reshape(f32[16,16,128]{2,1,0:T(8,128)S(1)} %copy-done.2) | data formatting | bytes 262144 | tf_op jit(solution)/shard_map/reshape | solution.py:81
  149.7 4.0 %reduce_sum.48 = f32[8,8,64]{2,1,0:T(8,128)S(1)} reduce(f32[8,2,8,2,64,2]{5,4,3,2,1,0:T(8,128)} %reshape.32, f32[]{:T(128)} %constant.7.clone.1), dimensions={1,3,5}, to_apply=%region_3.4 | reduce | flops 28672 | bytes 147460 | tf_op jit(solution)/shard_map/reduce_sum | solution.py:82
  163.2 3.9 %all-to-all-start.8 = ((f32[16,16,128]{2,1,0:T(8,128)}), f32[16,16,128]{2,1,0:T(8,128)}, u32[]{:S(2)}, u32[]{:S(2)}) async-start(f32[16,16,128]{2,1,0:T(8,128)} %fusion.17), calls=%async_computation.8 | async-start | bytes 262144 | tf_op jit(solution)/shard_map/all_to_all | solution.py:125
  167.2 9.7 %reshape.33 = f32[8,2,8,2,64,2]{5,4,3,2,1,0:T(8,128)} reshape(f32[16,16,128]{2,1,0:T(8,128)S(1)} %copy-done.51) | data formatting | bytes 262144 | tf_op jit(solution)/shard_map/reshape | solution.py:81
  176.9 9.7 %reshape.30 = f32[8,2,8,2,64,2]{5,4,3,2,1,0:T(8,128)} reshape(f32[16,16,128]{2,1,0:T(8,128)S(1)} %copy-done.1) | data formatting | bytes 262144 | tf_op jit(solution)/shard_map/reshape | solution.py:81
  186.6 4.6 %reduce_sum.49 = f32[8,8,64]{2,1,0:T(8,128)} reduce(f32[8,2,8,2,64,2]{5,4,3,2,1,0:T(8,128)} %reshape.33, f32[]{:T(128)} %constant.7.clone.1), dimensions={1,3,5}, to_apply=%region_4.5 | reduce | flops 28672 | bytes 147460 | tf_op jit(solution)/shard_map/reduce_sum | solution.py:82
  192.0 23.2 %all_gather.18 = f32[8,8,256]{1,0,2:T(8,128)S(1)} all-gather(f32[8,8,64]{1,0,2:T(8,128)} %copy.213), channel_id=1, replica_groups=mesh['gx'=4,'gy'=8] {'gx'}, dimensions={2}, use_global_device_ids=true | all-gather | bytes 81920 | tf_op jit(solution)/shard_map/all_gather | solution.py:161
  216.2 4.7 %reduce_sum.46 = f32[8,8,64]{2,1,0:T(8,128)} reduce(f32[8,2,8,2,64,2]{5,4,3,2,1,0:T(8,128)} %reshape.30, f32[]{:T(128)} %constant.7.clone.1), dimensions={1,3,5}, to_apply=%region_1.2 | reduce | flops 28672 | bytes 147460 | tf_op jit(solution)/shard_map/reduce_sum | solution.py:82
  226.7 4.3 %all-to-all-start.9 = ((f32[4,1,8192]{2,1,0:T(1,128)}), f32[4,1,8192]{2,1,0:T(1,128)S(1)}, u32[]{:S(2)}, u32[]{:S(2)}) async-start(f32[4,1,8192]{2,1,0:T(1,128)} %reshape.36), calls=%async_computation.9 | async-start | bytes 262144 | tf_op jit(solution)/shard_map/all_to_all | solution.py:90
  232.6 4.4 %all-to-all-done.9 = f32[4,1,8192]{2,1,0:T(1,128)S(1)} async-done(((f32[4,1,8192]{2,1,0:T(1,128)}), f32[4,1,8192]{2,1,0:T(1,128)S(1)}, u32[]{:S(2)}, u32[]{:S(2)}) %all-to-all-start.9) | async-done | bytes 131104 | tf_op jit(solution)/shard_map/all_to_all | solution.py:90
  244.9 4.4 %collective-permute-done.9 = f32[16,16,1]{2,1,0:T(8,128)S(1)} collective-permute-done((f32[16,16,1]{2,1,0:T(8,128)S(1)}, f32[16,16,1]{2,1,0:T(8,128)S(1)}, u32[]{:S(2)}, u32[]{:S(2)}) %collective-permute-start.9) | collective-permute-done | bytes 1056 | tf_op jit(solution)/shard_map/ppermute | solution.py:18
  263.4 4.8 %all-to-all-start.11 = ((f32[2,128,128]{2,0,1:T(2,128)}), f32[2,128,128]{2,0,1:T(2,128)S(1)}, u32[]{:S(2)}, u32[]{:S(2)}) async-start(f32[2,128,128]{2,0,1:T(2,128)} %copy.200), calls=%async_computation.11 | async-start | bytes 262144 | tf_op jit(solution)/shard_map/all_to_all | solution.py:94
  270.0 21.7 %all_gather.19 = f32[8,8,256]{1,0,2:T(8,128)S(1)} all-gather(f32[8,8,64]{1,0,2:T(8,128)S(1)} %copy.215), channel_id=1, replica_groups=mesh['gx'=4,'gy'=8] {'gx'}, dimensions={2}, use_global_device_ids=true | all-gather | bytes 81920 | tf_op jit(solution)/shard_map/all_gather | solution.py:162
  293.7 4.5 %collective-permute-start.11 = (f32[16,1,128]{2,1,0:T(1,128)S(1)}, f32[16,1,128]{2,1,0:T(1,128)S(1)}, u32[]{:S(2)}, u32[]{:S(2)}) collective-permute-start(f32[16,1,128]{2,1,0:T(1,128)S(1)} %get-tuple-element.84), channel_id=1, source_target_pairs={{1,0},{2,1},{3,2},{4,3},{5,4},{6,5},{7,6},{9,8},{10,9},{11,10},{12... | collective-permute-start | bytes 24584 | tf_op jit(solution)/shard_map/ppermute | solution.py:18
  298.2 20.6 %all_gather.16 = f32[8,8,256]{1,0,2:T(8,128)} all-gather(f32[8,8,64]{1,0,2:T(8,128)S(1)} %copy.205), channel_id=1, replica_groups=mesh['gx'=4,'gy'=8] {'gx'}, dimensions={2}, use_global_device_ids=true | all-gather | bytes 81920 | tf_op jit(solution)/shard_map/all_gather | solution.py:159
  328.3 4.4 %collective-permute-done.13 = f32[16,18,1]{2,1,0:T(8,128)S(1)} collective-permute-done((f32[16,18,1]{2,1,0:T(8,128)S(1)}, f32[16,18,1]{2,1,0:T(8,128)S(1)}, u32[]{:S(2)}, u32[]{:S(2)}) %collective-permute-start.13) | collective-permute-done | bytes 1184 | tf_op jit(solution)/shard_map/ppermute | solution.py:18
  333.9 9.7 %reshape.29 = f32[8,2,8,2,64,2]{5,4,3,2,1,0:T(8,128)} reshape(f32[16,16,128]{2,1,0:T(8,128)S(1)} %fusion.3) | data formatting | bytes 262144 | tf_op jit(solution)/shard_map/reshape | solution.py:81
  343.6 4.0 %reduce_sum.45 = f32[8,8,64]{2,1,0:T(8,128)S(1)} reduce(f32[8,2,8,2,64,2]{5,4,3,2,1,0:T(8,128)} %reshape.29, f32[]{:T(128)} %constant.7.clone.1), dimensions={1,3,5}, to_apply=%region_0.1 | reduce | flops 28672 | bytes 147460 | tf_op jit(solution)/shard_map/reduce_sum | solution.py:82
  347.8 19.2 %all_gather.15 = f32[8,8,256]{1,0,2:T(8,128)S(1)} all-gather(f32[8,8,64]{1,0,2:T(8,128)S(1)} %copy.203), channel_id=1, replica_groups=mesh['gx'=4,'gy'=8] {'gx'}, dimensions={2}, use_global_device_ids=true | all-gather | bytes 81920 | tf_op jit(solution)/shard_map/all_gather | solution.py:158
  (422 shorter events, 120.3 us)
Async XLA Ops:
  0.6 25.7 %all-to-all-start.1 = ((f32[16,16,128]{2,1,0:T(8,128)}), f32[16,16,128]{2,1,0:T(8,128)S(1)}, u32[]{:S(2)}, u32[]{:S(2)}) async-start(f32[16,16,128]{2,1,0:T(8,128)} %param.8), calls=%async_computation.1 | async-start | bytes 262144 | tf_op jit(solution)/shard_map/all_to_all | solution.py:127
  6.4 17.8 %collective-permute-start.2 = (f32[16,1,128]{2,1,0:T(1,128)S(1)}, f32[16,1,128]{2,1,0:T(1,128)S(1)}, u32[]{:S(2)}, u32[]{:S(2)}) collective-permute-start(f32[16,1,128]{2,1,0:T(1,128)S(1)} %get-tuple-element.265), channel_id=1, source_target_pairs={{0,1},{1,2},{2,3},{3,4},{4,5},{5,6},{6,7},{8,9},{9,10},{10,11},{11... | collective-permute-start | bytes 24584 | tf_op jit(solution)/shard_map/ppermute | solution.py:17
  8.3 15.9 %collective-permute-start.3 = (f32[16,1,128]{2,1,0:T(1,128)S(1)}, f32[16,1,128]{2,1,0:T(1,128)S(1)}, u32[]{:S(2)}, u32[]{:S(2)}) collective-permute-start(f32[16,1,128]{2,1,0:T(1,128)S(1)} %get-tuple-element.266), channel_id=1, source_target_pairs={{1,0},{2,1},{3,2},{4,3},{5,4},{6,5},{7,6},{9,8},{10,9},{11,10},{12... | collective-permute-start | bytes 24584 | tf_op jit(solution)/shard_map/ppermute | solution.py:18
  13.7 10.5 %collective-permute-start.1 = (f32[16,1,128]{2,1,0:T(1,128)S(1)}, f32[16,1,128]{2,1,0:T(1,128)S(1)}, u32[]{:S(2)}, u32[]{:S(2)}) collective-permute-start(f32[16,1,128]{2,1,0:T(1,128)S(1)} %slice.763), channel_id=1, source_target_pairs={{0,1},{1,2},{2,3},{3,4},{4,5},{5,6},{6,7},{8,9},{9,10},{10,11},{11... | collective-permute-start | bytes 24584 | tf_op jit(solution)/shard_map/ppermute | solution.py:26
  16.6 7.5 %collective-permute-start = (f32[16,16,1]{2,1,0:T(8,128)S(1)}, f32[16,16,1]{2,1,0:T(8,128)S(1)}, u32[]{:S(2)}, u32[]{:S(2)}) collective-permute-start(f32[16,16,1]{2,1,0:T(8,128)S(1)} %slice.761), channel_id=1, source_target_pairs={{0,8},{8,16},{16,24},{1,9},{9,17},{17,25},{2,10},{10,18},{18,26},{... | collective-permute-start | bytes 3080 | tf_op jit(solution)/shard_map/ppermute | solution.py:26
  26.4 69.7 %copy-start.15 = (f32[16,16,128]{2,1,0:T(8,128)}, f32[16,16,128]{2,1,0:T(8,128)S(1)}, u32[]{:S(2)}) copy-start(f32[16,16,128]{2,1,0:T(8,128)S(1)} %get-tuple-element.77) | copy-start | bytes 393220
  37.8 9.2 %all-to-all-start.2 = ((f32[16,16,128]{2,1,0:T(8,128)}), f32[16,16,128]{2,1,0:T(8,128)S(1)}, u32[]{:S(2)}, u32[]{:S(2)}) async-start(f32[16,16,128]{2,1,0:T(8,128)} %get-tuple-element.76), calls=%async_computation.2 | async-start | bytes 262144 | tf_op jit(solution)/shard_map/all_to_all | solution.py:126
  47.0 9.6 %all-to-all-start.5 = ((f32[16,16,128]{2,1,0:T(8,128)}), f32[16,16,128]{2,1,0:T(8,128)S(1)}, u32[]{:S(2)}, u32[]{:S(2)}) async-start(f32[16,16,128]{2,1,0:T(8,128)} %param.9), calls=%async_computation.5 | async-start | bytes 262144 | tf_op jit(solution)/shard_map/all_to_all | solution.py:140
  56.7 8.2 %all-to-all-start.6 = ((f32[16,16,128]{2,1,0:T(8,128)}), f32[16,16,128]{2,1,0:T(8,128)S(1)}, u32[]{:S(2)}, u32[]{:S(2)}) async-start(f32[16,16,128]{2,1,0:T(8,128)} %get-tuple-element.76), calls=%async_computation.6 | async-start | bytes 262144 | tf_op jit(solution)/shard_map/all_to_all | solution.py:139
  64.9 17.9 %all-to-all-start.3 = ((f32[4,1,8192]{2,1,0:T(1,128)}), f32[4,1,8192]{2,1,0:T(1,128)S(1)}, u32[]{:S(2)}, u32[]{:S(2)}) async-start(f32[4,1,8192]{2,1,0:T(1,128)} %reshape.34), calls=%async_computation.3 | async-start | bytes 262144 | tf_op jit(solution)/shard_map/all_to_all | solution.py:90
  85.4 6.4 %collective-permute-start.4 = (f32[16,16,1]{2,1,0:T(8,128)S(1)}, f32[16,16,1]{2,1,0:T(8,128)S(1)}, u32[]{:S(2)}, u32[]{:S(2)}) collective-permute-start(f32[16,16,1]{2,1,0:T(8,128)S(1)} %get-tuple-element.186), channel_id=1, source_target_pairs={{0,8},{8,16},{16,24},{1,9},{9,17},{17,25},{2,10},{10,18},{18,26},{... | collective-permute-start | bytes 3080 | tf_op jit(solution)/shard_map/ppermute | solution.py:17
  89.2 6.9 %collective-permute-start.5 = (f32[16,16,1]{2,1,0:T(8,128)S(1)}, f32[16,16,1]{2,1,0:T(8,128)S(1)}, u32[]{:S(2)}, u32[]{:S(2)}) collective-permute-start(f32[16,16,1]{2,1,0:T(8,128)S(1)} %get-tuple-element.187), channel_id=1, source_target_pairs={{8,0},{16,8},{24,16},{9,1},{17,9},{25,17},{10,2},{18,10},{26,18},{... | collective-permute-start | bytes 3080 | tf_op jit(solution)/shard_map/ppermute | solution.py:18
  97.0 8.8 %all-to-all-start.4 = ((f32[16,16,128]{2,1,0:T(8,128)}), f32[16,16,128]{2,1,0:T(8,128)S(1)}, u32[]{:S(2)}, u32[]{:S(2)}) async-start(f32[16,16,128]{2,1,0:T(8,128)} %fusion.22), calls=%async_computation.4 | async-start | bytes 262144 | tf_op jit(solution)/shard_map/all_to_all | solution.py:138
  109.7 44.0 %all-to-all-start.7 = ((f32[2,128,128]{2,0,1:T(2,128)}), f32[2,128,128]{2,0,1:T(2,128)}, u32[]{:S(2)}, u32[]{:S(2)}) async-start(f32[2,128,128]{2,0,1:T(2,128)} %copy.192), calls=%async_computation.7 | async-start | bytes 262144 | tf_op jit(solution)/shard_map/all_to_all | solution.py:94
  137.9 184.1 %collective-permute-start.14 = (f32[8,1,256]{2,0,1:T(8,128)S(1)}, f32[8,1,256]{2,0,1:T(8,128)}, u32[]{:S(2)}, u32[]{:S(2)}) collective-permute-start(f32[8,1,256]{2,0,1:T(8,128)S(1)} %copy.209), channel_id=1, source_target_pairs={{0,1},{1,2},{2,3},{3,4},{4,5},{5,6},{6,7},{8,9},{9,10},{10,11},{11... | collective-permute-start | bytes 24584 | tf_op jit(solution)/shard_map/ppermute | solution.py:26
  154.6 6.5 %collective-permute-start.6 = (f32[16,1,128]{2,1,0:T(1,128)S(1)}, f32[16,1,128]{2,1,0:T(1,128)S(1)}, u32[]{:S(2)}, u32[]{:S(2)}) collective-permute-start(f32[16,1,128]{2,1,0:T(1,128)S(1)} %get-tuple-element.123), channel_id=1, source_target_pairs={{0,1},{1,2},{2,3},{3,4},{4,5},{5,6},{6,7},{8,9},{9,10},{10,11},{11... | collective-permute-start | bytes 24584 | tf_op jit(solution)/shard_map/ppermute | solution.py:17
  158.1 4.3 %collective-permute-start.7 = (f32[16,1,128]{2,1,0:T(1,128)S(1)}, f32[16,1,128]{2,1,0:T(1,128)S(1)}, u32[]{:S(2)}, u32[]{:S(2)}) collective-permute-start(f32[16,1,128]{2,1,0:T(1,128)S(1)} %get-tuple-element.124), channel_id=1, source_target_pairs={{1,0},{2,1},{3,2},{4,3},{5,4},{6,5},{7,6},{9,8},{10,9},{11,10},{12... | collective-permute-start | bytes 24584 | tf_op jit(solution)/shard_map/ppermute | solution.py:18
  163.2 57.7 %all-to-all-start.8 = ((f32[16,16,128]{2,1,0:T(8,128)}), f32[16,16,128]{2,1,0:T(8,128)}, u32[]{:S(2)}, u32[]{:S(2)}) async-start(f32[16,16,128]{2,1,0:T(8,128)} %fusion.17), calls=%async_computation.8 | async-start | bytes 262144 | tf_op jit(solution)/shard_map/all_to_all | solution.py:125
  226.7 10.2 %all-to-all-start.9 = ((f32[4,1,8192]{2,1,0:T(1,128)}), f32[4,1,8192]{2,1,0:T(1,128)S(1)}, u32[]{:S(2)}, u32[]{:S(2)}) async-start(f32[4,1,8192]{2,1,0:T(1,128)} %reshape.36), calls=%async_computation.9 | async-start | bytes 262144 | tf_op jit(solution)/shard_map/all_to_all | solution.py:90
  239.1 5.8 %collective-permute-start.8 = (f32[16,16,1]{2,1,0:T(8,128)S(1)}, f32[16,16,1]{2,1,0:T(8,128)S(1)}, u32[]{:S(2)}, u32[]{:S(2)}) collective-permute-start(f32[16,16,1]{2,1,0:T(8,128)S(1)} %get-tuple-element.101), channel_id=1, source_target_pairs={{0,8},{8,16},{16,24},{1,9},{9,17},{17,25},{2,10},{10,18},{18,26},{... | collective-permute-start | bytes 3080 | tf_op jit(solution)/shard_map/ppermute | solution.py:17
  242.4 6.9 %collective-permute-start.9 = (f32[16,16,1]{2,1,0:T(8,128)S(1)}, f32[16,16,1]{2,1,0:T(8,128)S(1)}, u32[]{:S(2)}, u32[]{:S(2)}) collective-permute-start(f32[16,16,1]{2,1,0:T(8,128)S(1)} %get-tuple-element.102), channel_id=1, source_target_pairs={{8,0},{16,8},{24,16},{9,1},{17,9},{25,17},{10,2},{18,10},{26,18},{... | collective-permute-start | bytes 3080 | tf_op jit(solution)/shard_map/ppermute | solution.py:18
  251.0 7.3 %all-to-all-start.10 = ((f32[16,16,128]{2,1,0:T(8,128)}), f32[16,16,128]{2,1,0:T(8,128)S(1)}, u32[]{:S(2)}, u32[]{:S(2)}) async-start(f32[16,16,128]{2,1,0:T(8,128)} %fusion.12), calls=%async_computation.10 | async-start | bytes 262144 | tf_op jit(solution)/shard_map/all_to_all | solution.py:138
  259.3 73.4 %copy-start.16 = (f32[16,16,128]{2,1,0:T(8,128)S(1)}, f32[16,16,128]{2,1,0:T(8,128)}, u32[]{:S(2)}) copy-start(f32[16,16,128]{2,1,0:T(8,128)} %copy-done.15) | copy-start | bytes 393220
  263.4 28.3 %all-to-all-start.11 = ((f32[2,128,128]{2,0,1:T(2,128)}), f32[2,128,128]{2,0,1:T(2,128)S(1)}, u32[]{:S(2)}, u32[]{:S(2)}) async-start(f32[2,128,128]{2,0,1:T(2,128)} %copy.200), calls=%async_computation.11 | async-start | bytes 262144 | tf_op jit(solution)/shard_map/all_to_all | solution.py:94
  291.8 30.9 %collective-permute-start.10 = (f32[16,1,128]{2,1,0:T(1,128)S(1)}, f32[16,1,128]{2,1,0:T(1,128)S(1)}, u32[]{:S(2)}, u32[]{:S(2)}) collective-permute-start(f32[16,1,128]{2,1,0:T(1,128)S(1)} %get-tuple-element.83), channel_id=1, source_target_pairs={{0,1},{1,2},{2,3},{3,4},{4,5},{5,6},{6,7},{8,9},{9,10},{10,11},{11... | collective-permute-start | bytes 24584 | tf_op jit(solution)/shard_map/ppermute | solution.py:17
  293.7 29.0 %collective-permute-start.11 = (f32[16,1,128]{2,1,0:T(1,128)S(1)}, f32[16,1,128]{2,1,0:T(1,128)S(1)}, u32[]{:S(2)}, u32[]{:S(2)}) collective-permute-start(f32[16,1,128]{2,1,0:T(1,128)S(1)} %get-tuple-element.84), channel_id=1, source_target_pairs={{1,0},{2,1},{3,2},{4,3},{5,4},{6,5},{7,6},{9,8},{10,9},{11,10},{12... | collective-permute-start | bytes 24584 | tf_op jit(solution)/shard_map/ppermute | solution.py:18
  322.8 5.5 %collective-permute-start.12 = (f32[16,18,1]{2,1,0:T(8,128)S(1)}, f32[16,18,1]{2,1,0:T(8,128)S(1)}, u32[]{:S(2)}, u32[]{:S(2)}) collective-permute-start(f32[16,18,1]{2,1,0:T(8,128)S(1)} %get-tuple-element.79), channel_id=1, source_target_pairs={{0,8},{8,16},{16,24},{1,9},{9,17},{17,25},{2,10},{10,18},{18,26},{... | collective-permute-start | bytes 3464 | tf_op jit(solution)/shard_map/ppermute | solution.py:17
  325.1 7.6 %collective-permute-start.13 = (f32[16,18,1]{2,1,0:T(8,128)S(1)}, f32[16,18,1]{2,1,0:T(8,128)S(1)}, u32[]{:S(2)}, u32[]{:S(2)}) collective-permute-start(f32[16,18,1]{2,1,0:T(8,128)S(1)} %get-tuple-element.80), channel_id=1, source_target_pairs={{8,0},{16,8},{24,16},{9,1},{17,9},{25,17},{10,2},{18,10},{26,18},{... | collective-permute-start | bytes 3464 | tf_op jit(solution)/shard_map/ppermute | solution.py:18
  367.6 4.4 %collective-permute-start.16 = (f32[8,1,256]{2,0,1:T(8,128)S(1)}, f32[8,1,256]{2,0,1:T(8,128)S(1)}, u32[]{:S(2)}, u32[]{:S(2)}) collective-permute-start(f32[8,1,256]{2,0,1:T(8,128)S(1)} %copy.220), channel_id=1, source_target_pairs={{1,0},{2,1},{3,2},{4,3},{5,4},{6,5},{7,6},{9,8},{10,9},{11,10},{12... | collective-permute-start | bytes 24584 | tf_op jit(solution)/shard_map/ppermute | solution.py:18
  369.6 5.9 %collective-permute-start.15 = (f32[8,1,256]{2,0,1:T(8,128)S(1)}, f32[8,1,256]{2,0,1:T(8,128)S(1)}, u32[]{:S(2)}, u32[]{:S(2)}) collective-permute-start(f32[8,1,256]{2,0,1:T(8,128)S(1)} %copy.218), channel_id=1, source_target_pairs={{0,1},{1,2},{2,3},{3,4},{4,5},{5,6},{6,7},{8,9},{9,10},{10,11},{11... | collective-permute-start | bytes 24584 | tf_op jit(solution)/shard_map/ppermute | solution.py:17
  375.7 4.4 %collective-permute-start.18 = (f32[8,1,256]{2,0,1:T(8,128)S(1)}, f32[8,1,256]{2,0,1:T(8,128)S(1)}, u32[]{:S(2)}, u32[]{:S(2)}) collective-permute-start(f32[8,1,256]{2,0,1:T(8,128)S(1)} %copy.227), channel_id=1, source_target_pairs={{1,0},{2,1},{3,2},{4,3},{5,4},{6,5},{7,6},{9,8},{10,9},{11,10},{12... | collective-permute-start | bytes 24584 | tf_op jit(solution)/shard_map/ppermute | solution.py:18
  377.6 5.9 %collective-permute-start.17 = (f32[8,1,256]{2,0,1:T(8,128)S(1)}, f32[8,1,256]{2,0,1:T(8,128)S(1)}, u32[]{:S(2)}, u32[]{:S(2)}) collective-permute-start(f32[8,1,256]{2,0,1:T(8,128)S(1)} %copy.225), channel_id=1, source_target_pairs={{0,1},{1,2},{2,3},{3,4},{4,5},{5,6},{6,7},{8,9},{9,10},{10,11},{11... | collective-permute-start | bytes 24584 | tf_op jit(solution)/shard_map/ppermute | solution.py:17
  (78 other events, 1003.7 us)
where the time goes:
time: 387 us; the launch traced here: 384 us
  blocking collectives  118 us (30%)
  starting transfers between devices  95.2 us (25%)
  local copies, waits for them, and re-layouts  77.1 us (20%)
  other arithmetic  45.6 us (12%)
  waiting for transfers between devices  45.5 us (12%)
    reshape x5, local copies, waits for them, and re-layouts, restrict(): blocks = field.reshape(levels // 2, 2, rows // 2, 2, columns // 2, 2)  48.6 us
    all_gather x1, blocking collectives, body(): lax.all_gather(coarse_z, 'gx', axis=2, tiled=True)  23.2 us
    reduce_sum x5, other arithmetic, restrict(): return jnp.sum(blocks, axis=(1, 3, 5)) * 0.125  22 us
    all_gather x1, blocking collectives, body(): lax.all_gather(coarse_y, 'gx', axis=2, tiled=True)  21.7 us
    all_gather x1, blocking collectives, body(): lax.all_gather(coarse_damp, 'gx', axis=2, tiled=True)  21.7 us
    ppermute x8, starting transfers between devices, extended(): before = lax.ppermute(last, axis, up)  21.6 us
    all_gather x1, blocking collectives, body(): lax.all_gather(coarse_x, 'gx', axis=2, tiled=True)  20.6 us
    ppermute x8, starting transfers between devices, extended(): after = lax.ppermute(leading, axis, down)  19.8 us
  transfers between devices with their start and end apart: 30, of which 15 were waited for; matrix products, arithmetic and copies ran while one was open for 26% of the time, Pallas kernels for 0%

commit v1 on v0

--- a/solution.py
+++ b/solution.py
@@ -158,7 +158,7 @@
         lax.all_gather(coarse_residual, "gx", axis=2, tiled=True),
         lax.all_gather(coarse_x, "gx", axis=2, tiled=True),
         lax.all_gather(coarse_y, "gx", axis=2, tiled=True),
-        lax.all_gather(coarse_z, "gx", axis=2, tiled=True),
+        jnp.concatenate(lax.all_gather(coarse_z, "gx"), axis=2),
         lax.all_gather(coarse_damp, "gx", axis=2, tiled=True),
     )
     cz_top = top_masked(whole_z)

time: 387 us -> 380 us (0.982)
  blocking collectives: 118 us -> 109 us
    all_gather x1, blocking collectives: 23.2 us -> 14.1 us  [body(): lax.all_gather(coarse_z, 'gx')]
where the time goes in v1:
time: 380 us; the launch traced here: 378 us
  blocking collectives  109 us (29%)
  starting transfers between devices  94.9 us (25%)
  local copies, waits for them, and re-layouts  76.8 us (20%)
  other arithmetic  48.9 us (13%)
  waiting for transfers between devices  45.5 us (12%)
    reshape x5, local copies, waits for them, and re-layouts, restrict(): blocks = field.reshape(levels // 2, 2, rows // 2, 2, columns // 2, 2)  48.6 us
    reduce_sum x5, other arithmetic, restrict(): return jnp.sum(blocks, axis=(1, 3, 5)) * 0.125  22 us
    all_gather x1, blocking collectives, body(): lax.all_gather(coarse_y, 'gx', axis=2, tiled=True)  21.7 us
    all_gather x1, blocking collectives, body(): lax.all_gather(coarse_damp, 'gx', axis=2, tiled=True)  21.7 us
    ppermute x8, starting transfers between devices, extended(): before = lax.ppermute(last, axis, up)  21.6 us
    all_gather x1, blocking collectives, body(): lax.all_gather(coarse_x, 'gx', axis=2, tiled=True)  20.6 us
    ppermute x8, starting transfers between devices, extended(): after = lax.ppermute(leading, axis, down)  19.8 us
    all_gather x1, blocking collectives, body(): lax.all_gather(coarse_residual, 'gx', axis=2, tiled=True)  19.2 us
  transfers between devices with their start and end apart: 30, of which 15 were waited for; matrix products, arithmetic and copies ran while one was open for 26% of the time, Pallas kernels for 0%

profile of v1, /device:TPU:4, one launch (start us, length us, event | category | flops | bytes accessed | tf_op | source)
XLA Modules:
  0.0 377.7 jit_solution(6967750471538641045)
XLA Ops:
  0.6 4.9 %all-to-all-start.1 = ((f32[16,16,128]{2,1,0:T(8,128)}), f32[16,16,128]{2,1,0:T(8,128)S(1)}, u32[]{:S(2)}, u32[]{:S(2)}) async-start(f32[16,16,128]{2,1,0:T(8,128)} %param.8), calls=%async_computation.1 | async-start | bytes 262144 | tf_op jit(solution)/shard_map/all_to_all | solution.py:127
  8.3 4.5 %collective-permute-start.3 = (f32[16,1,128]{2,1,0:T(1,128)S(1)}, f32[16,1,128]{2,1,0:T(1,128)S(1)}, u32[]{:S(2)}, u32[]{:S(2)}) collective-permute-start(f32[16,1,128]{2,1,0:T(1,128)S(1)} %get-tuple-element.266), channel_id=1, source_target_pairs={{1,0},{2,1},{3,2},{4,3},{5,4},{6,5},{7,6},{9,8},{10,9},{11,10},{12... | collective-permute-start | bytes 24584 | tf_op jit(solution)/shard_map/ppermute | solution.py:18
  16.6 3.9 %collective-permute-start = (f32[16,16,1]{2,1,0:T(8,128)S(1)}, f32[16,16,1]{2,1,0:T(8,128)S(1)}, u32[]{:S(2)}, u32[]{:S(2)}) collective-permute-start(f32[16,16,1]{2,1,0:T(8,128)S(1)} %slice.761), channel_id=1, source_target_pairs={{0,8},{8,16},{16,24},{1,9},{9,17},{17,25},{2,10},{10,18},{18,26},{... | collective-permute-start | bytes 3080 | tf_op jit(solution)/shard_map/ppermute | solution.py:26
  26.4 11.4 %all_to_all.236 = f32[16,16,128]{2,1,0:T(8,128)S(1)} all-to-all(f32[16,16,128]{2,1,0:T(8,128)S(1)} %get-tuple-element.78), channel_id=1, replica_groups=mesh['gx'=4,'gy'=8] {'gx'}, dimensions={0} | all-to-all | bytes 262144 | tf_op jit(solution)/shard_map/all_to_all | solution.py:125
  41.4 5.6 %all-to-all-done.2 = f32[16,16,128]{2,1,0:T(8,128)S(1)} async-done(((f32[16,16,128]{2,1,0:T(8,128)}), f32[16,16,128]{2,1,0:T(8,128)S(1)}, u32[]{:S(2)}, u32[]{:S(2)}) %all-to-all-start.2) | async-done | bytes 131104 | tf_op jit(solution)/shard_map/all_to_all | solution.py:126
  56.6 4.2 %all-to-all-start.6 = ((f32[16,16,128]{2,1,0:T(8,128)}), f32[16,16,128]{2,1,0:T(8,128)S(1)}, u32[]{:S(2)}, u32[]{:S(2)}) async-start(f32[16,16,128]{2,1,0:T(8,128)} %get-tuple-element.76), calls=%async_computation.6 | async-start | bytes 262144 | tf_op jit(solution)/shard_map/all_to_all | solution.py:139
  68.2 9.7 %reshape.46 = f32[8,2,8,2,64,2]{5,4,3,2,1,0:T(8,128)} reshape(f32[16,16,128]{2,1,0:T(8,128)S(1)} %copy-done) | data formatting | bytes 262144 | tf_op jit(solution)/shard_map/reshape | solution.py:81
  78.0 4.7 %reduce_sum.47 = f32[8,8,64]{2,1,0:T(8,128)} reduce(f32[8,2,8,2,64,2]{5,4,3,2,1,0:T(8,128)} %reshape.46, f32[]{:T(128)} %constant.7.clone.1), dimensions={1,3,5}, to_apply=%region_2.3 | reduce | flops 28672 | bytes 147460 | tf_op jit(solution)/shard_map/reduce_sum | solution.py:82
  85.5 3.9 %collective-permute-start.4 = (f32[16,16,1]{2,1,0:T(8,128)S(1)}, f32[16,16,1]{2,1,0:T(8,128)S(1)}, u32[]{:S(2)}, u32[]{:S(2)}) collective-permute-start(f32[16,16,1]{2,1,0:T(8,128)S(1)} %get-tuple-element.186), channel_id=1, source_target_pairs={{0,8},{8,16},{16,24},{1,9},{9,17},{17,25},{2,10},{10,18},{18,26},{... | collective-permute-start | bytes 3080 | tf_op jit(solution)/shard_map/ppermute | solution.py:17
  91.9 4.4 %collective-permute-done.5 = f32[16,16,1]{2,1,0:T(8,128)S(1)} collective-permute-done((f32[16,16,1]{2,1,0:T(8,128)S(1)}, f32[16,16,1]{2,1,0:T(8,128)S(1)}, u32[]{:S(2)}, u32[]{:S(2)}) %collective-permute-start.5) | collective-permute-done | bytes 1056 | tf_op jit(solution)/shard_map/ppermute | solution.py:18
  97.2 4.8 %all-to-all-start.4 = ((f32[16,16,128]{2,1,0:T(8,128)}), f32[16,16,128]{2,1,0:T(8,128)S(1)}, u32[]{:S(2)}, u32[]{:S(2)}) async-start(f32[16,16,128]{2,1,0:T(8,128)} %fusion.22), calls=%async_computation.4 | async-start | bytes 262144 | tf_op jit(solution)/shard_map/all_to_all | solution.py:138
  101.9 4.0 %all-to-all-done.4 = f32[16,16,128]{2,1,0:T(8,128)S(1)} async-done(((f32[16,16,128]{2,1,0:T(8,128)}), f32[16,16,128]{2,1,0:T(8,128)S(1)}, u32[]{:S(2)}, u32[]{:S(2)}) %all-to-all-start.4) | async-done | bytes 131104 | tf_op jit(solution)/shard_map/all_to_all | solution.py:138
  109.9 5.6 %all-to-all-start.7 = ((f32[2,128,128]{2,0,1:T(2,128)}), f32[2,128,128]{2,0,1:T(2,128)}, u32[]{:S(2)}, u32[]{:S(2)}) async-start(f32[2,128,128]{2,0,1:T(2,128)} %copy.196), calls=%async_computation.7 | async-start | bytes 262144 | tf_op jit(solution)/shard_map/all_to_all | solution.py:94
  115.6 21.7 %all_gather.18 = f32[8,8,256]{1,0,2:T(8,128)S(1)} all-gather(f32[8,8,64]{1,0,2:T(8,128)S(1)} %copy.212), channel_id=1, replica_groups=mesh['gx'=4,'gy'=8] {'gx'}, dimensions={2}, use_global_device_ids=true | all-gather | bytes 81920 | tf_op jit(solution)/shard_map/all_gather | solution.py:160
  140.1 9.7 %reshape.47 = f32[8,2,8,2,64,2]{5,4,3,2,1,0:T(8,128)} reshape(f32[16,16,128]{2,1,0:T(8,128)S(1)} %copy-done.2) | data formatting | bytes 262144 | tf_op jit(solution)/shard_map/reshape | solution.py:81
  149.8 4.0 %reduce_sum.48 = f32[8,8,64]{2,1,0:T(8,128)S(1)} reduce(f32[8,2,8,2,64,2]{5,4,3,2,1,0:T(8,128)} %reshape.47, f32[]{:T(128)} %constant.7.clone.1), dimensions={1,3,5}, to_apply=%region_3.4 | reduce | flops 28672 | bytes 147460 | tf_op jit(solution)/shard_map/reduce_sum | solution.py:82
  166.7 9.7 %reshape.50 = f32[8,2,8,2,64,2]{5,4,3,2,1,0:T(8,128)} reshape(f32[16,16,128]{2,1,0:T(8,128)S(1)} %copy-done.47) | data formatting | bytes 262144 | tf_op jit(solution)/shard_map/reshape | solution.py:81
  176.4 9.7 %reshape.45 = f32[8,2,8,2,64,2]{5,4,3,2,1,0:T(8,128)} reshape(f32[16,16,128]{2,1,0:T(8,128)S(1)} %copy-done.1) | data formatting | bytes 262144 | tf_op jit(solution)/shard_map/reshape | solution.py:81
  186.1 4.7 %reduce_sum.49 = f32[8,8,64]{2,1,0:T(8,128)} reduce(f32[8,2,8,2,64,2]{5,4,3,2,1,0:T(8,128)} %reshape.50, f32[]{:T(128)} %constant.7.clone.1), dimensions={1,3,5}, to_apply=%region_4.5 | reduce | flops 28672 | bytes 147460 | tf_op jit(solution)/shard_map/reduce_sum | solution.py:82
  190.8 14.1 %all-gather = f32[32,8,64]{2,1,0:T(8,128)S(1)} all-gather(f32[8,8,64]{2,1,0:T(8,128)S(1)} %broadcast_multiply_fusion.1), channel_id=2, replica_groups=mesh['gx'=4,'gy'=8] {'gx'}, dimensions={0}, use_global_device_ids=true | all-gather | bytes 81920 | tf_op jit(solution)/shard_map/all_gather | solution.py:161
  205.7 4.6 %reduce_sum.46 = f32[8,8,64]{2,1,0:T(8,128)} reduce(f32[8,2,8,2,64,2]{5,4,3,2,1,0:T(8,128)} %reshape.45, f32[]{:T(128)} %constant.7.clone.1), dimensions={1,3,5}, to_apply=%region_1.2 | reduce | flops 28672 | bytes 147460 | tf_op jit(solution)/shard_map/reduce_sum | solution.py:82
  219.7 4.6 %all-to-all-start.9 = ((f32[4,1,8192]{2,1,0:T(1,128)}), f32[4,1,8192]{2,1,0:T(1,128)S(1)}, u32[]{:S(2)}, u32[]{:S(2)}) async-start(f32[4,1,8192]{2,1,0:T(1,128)} %reshape.54), calls=%async_computation.9 | async-start | bytes 262144 | tf_op jit(solution)/shard_map/all_to_all | solution.py:90
  225.9 4.4 %all-to-all-done.9 = f32[4,1,8192]{2,1,0:T(1,128)S(1)} async-done(((f32[4,1,8192]{2,1,0:T(1,128)}), f32[4,1,8192]{2,1,0:T(1,128)S(1)}, u32[]{:S(2)}, u32[]{:S(2)}) %all-to-all-start.9) | async-done | bytes 131104 | tf_op jit(solution)/shard_map/all_to_all | solution.py:90
  238.3 4.4 %collective-permute-done.9 = f32[16,16,1]{2,1,0:T(8,128)S(1)} collective-permute-done((f32[16,16,1]{2,1,0:T(8,128)S(1)}, f32[16,16,1]{2,1,0:T(8,128)S(1)}, u32[]{:S(2)}, u32[]{:S(2)}) %collective-permute-start.9) | collective-permute-done | bytes 1056 | tf_op jit(solution)/shard_map/ppermute | solution.py:18
  256.9 4.8 %all-to-all-start.11 = ((f32[2,128,128]{2,0,1:T(2,128)}), f32[2,128,128]{2,0,1:T(2,128)S(1)}, u32[]{:S(2)}, u32[]{:S(2)}) async-start(f32[2,128,128]{2,0,1:T(2,128)} %copy.204), calls=%async_computation.11 | async-start | bytes 262144 | tf_op jit(solution)/shard_map/all_to_all | solution.py:94
  263.4 21.7 %all_gather.20 = f32[8,8,256]{1,0,2:T(8,128)S(1)} all-gather(f32[8,8,64]{1,0,2:T(8,128)S(1)} %copy.218), channel_id=1, replica_groups=mesh['gx'=4,'gy'=8] {'gx'}, dimensions={2}, use_global_device_ids=true | all-gather | bytes 81920 | tf_op jit(solution)/shard_map/all_gather | solution.py:162
  287.1 4.5 %collective-permute-start.11 = (f32[16,1,128]{2,1,0:T(1,128)S(1)}, f32[16,1,128]{2,1,0:T(1,128)S(1)}, u32[]{:S(2)}, u32[]{:S(2)}) collective-permute-start(f32[16,1,128]{2,1,0:T(1,128)S(1)} %get-tuple-element.84), channel_id=1, source_target_pairs={{1,0},{2,1},{3,2},{4,3},{5,4},{6,5},{7,6},{9,8},{10,9},{11,10},{12... | collective-permute-start | bytes 24584 | tf_op jit(solution)/shard_map/ppermute | solution.py:18
  291.7 20.6 %all_gather.17 = f32[8,8,256]{1,0,2:T(8,128)} all-gather(f32[8,8,64]{1,0,2:T(8,128)S(1)} %copy.209), channel_id=1, replica_groups=mesh['gx'=4,'gy'=8] {'gx'}, dimensions={2}, use_global_device_ids=true | all-gather | bytes 81920 | tf_op jit(solution)/shard_map/all_gather | solution.py:159
  321.7 4.4 %collective-permute-done.13 = f32[16,18,1]{2,1,0:T(8,128)S(1)} collective-permute-done((f32[16,18,1]{2,1,0:T(8,128)S(1)}, f32[16,18,1]{2,1,0:T(8,128)S(1)}, u32[]{:S(2)}, u32[]{:S(2)}) %collective-permute-start.13) | collective-permute-done | bytes 1184 | tf_op jit(solution)/shard_map/ppermute | solution.py:18
  327.3 9.7 %reshape.44 = f32[8,2,8,2,64,2]{5,4,3,2,1,0:T(8,128)} reshape(f32[16,16,128]{2,1,0:T(8,128)S(1)} %fusion.3) | data formatting | bytes 262144 | tf_op jit(solution)/shard_map/reshape | solution.py:81
  337.0 4.0 %reduce_sum.45 = f32[8,8,64]{2,1,0:T(8,128)S(1)} reduce(f32[8,2,8,2,64,2]{5,4,3,2,1,0:T(8,128)} %reshape.44, f32[]{:T(128)} %constant.7.clone.1), dimensions={1,3,5}, to_apply=%region_0.1 | reduce | flops 28672 | bytes 147460 | tf_op jit(solution)/shard_map/reduce_sum | solution.py:82
  341.2 19.2 %all_gather.16 = f32[8,8,256]{1,0,2:T(8,128)S(1)} all-gather(f32[8,8,64]{1,0,2:T(8,128)S(1)} %copy.207), channel_id=1, replica_groups=mesh['gx'=4,'gy'=8] {'gx'}, dimensions={2}, use_global_device_ids=true | all-gather | bytes 81920 | tf_op jit(solution)/shard_map/all_gather | solution.py:158
  (402 shorter events, 122.7 us)
Async XLA Ops:
  0.6 25.7 %all-to-all-start.1 = ((f32[16,16,128]{2,1,0:T(8,128)}), f32[16,16,128]{2,1,0:T(8,128)S(1)}, u32[]{:S(2)}, u32[]{:S(2)}) async-start(f32[16,16,128]{2,1,0:T(8,128)} %param.8), calls=%async_computation.1 | async-start | bytes 262144 | tf_op jit(solution)/shard_map/all_to_all | solution.py:127
  6.4 17.8 %collective-permute-start.2 = (f32[16,1,128]{2,1,0:T(1,128)S(1)}, f32[16,1,128]{2,1,0:T(1,128)S(1)}, u32[]{:S(2)}, u32[]{:S(2)}) collective-permute-start(f32[16,1,128]{2,1,0:T(1,128)S(1)} %get-tuple-element.265), channel_id=1, source_target_pairs={{0,1},{1,2},{2,3},{3,4},{4,5},{5,6},{6,7},{8,9},{9,10},{10,11},{11... | collective-permute-start | bytes 24584 | tf_op jit(solution)/shard_map/ppermute | solution.py:17
  8.3 15.9 %collective-permute-start.3 = (f32[16,1,128]{2,1,0:T(1,128)S(1)}, f32[16,1,128]{2,1,0:T(1,128)S(1)}, u32[]{:S(2)}, u32[]{:S(2)}) collective-permute-start(f32[16,1,128]{2,1,0:T(1,128)S(1)} %get-tuple-element.266), channel_id=1, source_target_pairs={{1,0},{2,1},{3,2},{4,3},{5,4},{6,5},{7,6},{9,8},{10,9},{11,10},{12... | collective-permute-start | bytes 24584 | tf_op jit(solution)/shard_map/ppermute | solution.py:18
  13.7 10.5 %collective-permute-start.1 = (f32[16,1,128]{2,1,0:T(1,128)S(1)}, f32[16,1,128]{2,1,0:T(1,128)S(1)}, u32[]{:S(2)}, u32[]{:S(2)}) collective-permute-start(f32[16,1,128]{2,1,0:T(1,128)S(1)} %slice.763), channel_id=1, source_target_pairs={{0,1},{1,2},{2,3},{3,4},{4,5},{5,6},{6,7},{8,9},{9,10},{10,11},{11... | collective-permute-start | bytes 24584 | tf_op jit(solution)/shard_map/ppermute | solution.py:26
  16.6 7.5 %collective-permute-start = (f32[16,16,1]{2,1,0:T(8,128)S(1)}, f32[16,16,1]{2,1,0:T(8,128)S(1)}, u32[]{:S(2)}, u32[]{:S(2)}) collective-permute-start(f32[16,16,1]{2,1,0:T(8,128)S(1)} %slice.761), channel_id=1, source_target_pairs={{0,8},{8,16},{16,24},{1,9},{9,17},{17,25},{2,10},{10,18},{18,26},{... | collective-permute-start | bytes 3080 | tf_op jit(solution)/shard_map/ppermute | solution.py:26
  26.4 69.9 %copy-start.15 = (f32[16,16,128]{2,1,0:T(8,128)}, f32[16,16,128]{2,1,0:T(8,128)S(1)}, u32[]{:S(2)}) copy-start(f32[16,16,128]{2,1,0:T(8,128)S(1)} %get-tuple-element.77) | copy-start | bytes 393220
  37.8 9.2 %all-to-all-start.2 = ((f32[16,16,128]{2,1,0:T(8,128)}), f32[16,16,128]{2,1,0:T(8,128)S(1)}, u32[]{:S(2)}, u32[]{:S(2)}) async-start(f32[16,16,128]{2,1,0:T(8,128)} %get-tuple-element.76), calls=%async_computation.2 | async-start | bytes 262144 | tf_op jit(solution)/shard_map/all_to_all | solution.py:126
  47.0 9.6 %all-to-all-start.5 = ((f32[16,16,128]{2,1,0:T(8,128)}), f32[16,16,128]{2,1,0:T(8,128)S(1)}, u32[]{:S(2)}, u32[]{:S(2)}) async-start(f32[16,16,128]{2,1,0:T(8,128)} %param.9), calls=%async_computation.5 | async-start | bytes 262144 | tf_op jit(solution)/shard_map/all_to_all | solution.py:140
  56.6 8.2 %all-to-all-start.6 = ((f32[16,16,128]{2,1,0:T(8,128)}), f32[16,16,128]{2,1,0:T(8,128)S(1)}, u32[]{:S(2)}, u32[]{:S(2)}) async-start(f32[16,16,128]{2,1,0:T(8,128)} %get-tuple-element.76), calls=%async_computation.6 | async-start | bytes 262144 | tf_op jit(solution)/shard_map/all_to_all | solution.py:139
  64.9 17.9 %all-to-all-start.3 = ((f32[4,1,8192]{2,1,0:T(1,128)}), f32[4,1,8192]{2,1,0:T(1,128)S(1)}, u32[]{:S(2)}, u32[]{:S(2)}) async-start(f32[4,1,8192]{2,1,0:T(1,128)} %reshape.52), calls=%async_computation.3 | async-start | bytes 262144 | tf_op jit(solution)/shard_map/all_to_all | solution.py:90
  85.5 6.4 %collective-permute-start.4 = (f32[16,16,1]{2,1,0:T(8,128)S(1)}, f32[16,16,1]{2,1,0:T(8,128)S(1)}, u32[]{:S(2)}, u32[]{:S(2)}) collective-permute-start(f32[16,16,1]{2,1,0:T(8,128)S(1)} %get-tuple-element.186), channel_id=1, source_target_pairs={{0,8},{8,16},{16,24},{1,9},{9,17},{17,25},{2,10},{10,18},{18,26},{... | collective-permute-start | bytes 3080 | tf_op jit(solution)/shard_map/ppermute | solution.py:17
  89.4 6.9 %collective-permute-start.5 = (f32[16,16,1]{2,1,0:T(8,128)S(1)}, f32[16,16,1]{2,1,0:T(8,128)S(1)}, u32[]{:S(2)}, u32[]{:S(2)}) collective-permute-start(f32[16,16,1]{2,1,0:T(8,128)S(1)} %get-tuple-element.187), channel_id=1, source_target_pairs={{8,0},{16,8},{24,16},{9,1},{17,9},{25,17},{10,2},{18,10},{26,18},{... | collective-permute-start | bytes 3080 | tf_op jit(solution)/shard_map/ppermute | solution.py:18
  97.2 8.8 %all-to-all-start.4 = ((f32[16,16,128]{2,1,0:T(8,128)}), f32[16,16,128]{2,1,0:T(8,128)S(1)}, u32[]{:S(2)}, u32[]{:S(2)}) async-start(f32[16,16,128]{2,1,0:T(8,128)} %fusion.22), calls=%async_computation.4 | async-start | bytes 262144 | tf_op jit(solution)/shard_map/all_to_all | solution.py:138
  109.9 44.0 %all-to-all-start.7 = ((f32[2,128,128]{2,0,1:T(2,128)}), f32[2,128,128]{2,0,1:T(2,128)}, u32[]{:S(2)}, u32[]{:S(2)}) async-start(f32[2,128,128]{2,0,1:T(2,128)} %copy.196), calls=%async_computation.7 | async-start | bytes 262144 | tf_op jit(solution)/shard_map/all_to_all | solution.py:94
  138.0 177.3 %collective-permute-start.14 = (f32[8,1,256]{2,0,1:T(8,128)S(1)}, f32[8,1,256]{2,0,1:T(8,128)}, u32[]{:S(2)}, u32[]{:S(2)}) collective-permute-start(f32[8,1,256]{2,0,1:T(8,128)S(1)} %copy.213), channel_id=1, source_target_pairs={{0,1},{1,2},{2,3},{3,4},{4,5},{5,6},{6,7},{8,9},{9,10},{10,11},{11... | collective-permute-start | bytes 24584 | tf_op jit(solution)/shard_map/ppermute | solution.py:26
  154.8 6.5 %collective-permute-start.6 = (f32[16,1,128]{2,1,0:T(1,128)S(1)}, f32[16,1,128]{2,1,0:T(1,128)S(1)}, u32[]{:S(2)}, u32[]{:S(2)}) collective-permute-start(f32[16,1,128]{2,1,0:T(1,128)S(1)} %get-tuple-element.123), channel_id=1, source_target_pairs={{0,1},{1,2},{2,3},{3,4},{4,5},{5,6},{6,7},{8,9},{9,10},{10,11},{11... | collective-permute-start | bytes 24584 | tf_op jit(solution)/shard_map/ppermute | solution.py:17
  158.3 4.3 %collective-permute-start.7 = (f32[16,1,128]{2,1,0:T(1,128)S(1)}, f32[16,1,128]{2,1,0:T(1,128)S(1)}, u32[]{:S(2)}, u32[]{:S(2)}) collective-permute-start(f32[16,1,128]{2,1,0:T(1,128)S(1)} %get-tuple-element.124), channel_id=1, source_target_pairs={{1,0},{2,1},{3,2},{4,3},{5,4},{6,5},{7,6},{9,8},{10,9},{11,10},{12... | collective-permute-start | bytes 24584 | tf_op jit(solution)/shard_map/ppermute | solution.py:18
  163.4 47.0 %all-to-all-start.8 = ((f32[16,16,128]{2,1,0:T(8,128)}), f32[16,16,128]{2,1,0:T(8,128)S(1)}, u32[]{:S(2)}, u32[]{:S(2)}) async-start(f32[16,16,128]{2,1,0:T(8,128)} %fusion.17), calls=%async_computation.8 | async-start | bytes 262144 | tf_op jit(solution)/shard_map/all_to_all | solution.py:125
  219.7 10.6 %all-to-all-start.9 = ((f32[4,1,8192]{2,1,0:T(1,128)}), f32[4,1,8192]{2,1,0:T(1,128)S(1)}, u32[]{:S(2)}, u32[]{:S(2)}) async-start(f32[4,1,8192]{2,1,0:T(1,128)} %reshape.54), calls=%async_computation.9 | async-start | bytes 262144 | tf_op jit(solution)/shard_map/all_to_all | solution.py:90
  232.5 5.8 %collective-permute-start.8 = (f32[16,16,1]{2,1,0:T(8,128)S(1)}, f32[16,16,1]{2,1,0:T(8,128)S(1)}, u32[]{:S(2)}, u32[]{:S(2)}) collective-permute-start(f32[16,16,1]{2,1,0:T(8,128)S(1)} %get-tuple-element.101), channel_id=1, source_target_pairs={{0,8},{8,16},{16,24},{1,9},{9,17},{17,25},{2,10},{10,18},{18,26},{... | collective-permute-start | bytes 3080 | tf_op jit(solution)/shard_map/ppermute | solution.py:17
  235.8 6.9 %collective-permute-start.9 = (f32[16,16,1]{2,1,0:T(8,128)S(1)}, f32[16,16,1]{2,1,0:T(8,128)S(1)}, u32[]{:S(2)}, u32[]{:S(2)}) collective-permute-start(f32[16,16,1]{2,1,0:T(8,128)S(1)} %get-tuple-element.102), channel_id=1, source_target_pairs={{8,0},{16,8},{24,16},{9,1},{17,9},{25,17},{10,2},{18,10},{26,18},{... | collective-permute-start | bytes 3080 | tf_op jit(solution)/shard_map/ppermute | solution.py:18
  244.4 7.3 %all-to-all-start.10 = ((f32[16,16,128]{2,1,0:T(8,128)}), f32[16,16,128]{2,1,0:T(8,128)S(1)}, u32[]{:S(2)}, u32[]{:S(2)}) async-start(f32[16,16,128]{2,1,0:T(8,128)} %fusion.12), calls=%async_computation.10 | async-start | bytes 262144 | tf_op jit(solution)/shard_map/all_to_all | solution.py:138
  252.8 73.4 %copy-start.16 = (f32[16,16,128]{2,1,0:T(8,128)S(1)}, f32[16,16,128]{2,1,0:T(8,128)}, u32[]{:S(2)}) copy-start(f32[16,16,128]{2,1,0:T(8,128)} %copy-done.15) | copy-start | bytes 393220
  256.9 28.3 %all-to-all-start.11 = ((f32[2,128,128]{2,0,1:T(2,128)}), f32[2,128,128]{2,0,1:T(2,128)S(1)}, u32[]{:S(2)}, u32[]{:S(2)}) async-start(f32[2,128,128]{2,0,1:T(2,128)} %copy.204), calls=%async_computation.11 | async-start | bytes 262144 | tf_op jit(solution)/shard_map/all_to_all | solution.py:94
  285.2 30.9 %collective-permute-start.10 = (f32[16,1,128]{2,1,0:T(1,128)S(1)}, f32[16,1,128]{2,1,0:T(1,128)S(1)}, u32[]{:S(2)}, u32[]{:S(2)}) collective-permute-start(f32[16,1,128]{2,1,0:T(1,128)S(1)} %get-tuple-element.83), channel_id=1, source_target_pairs={{0,1},{1,2},{2,3},{3,4},{4,5},{5,6},{6,7},{8,9},{9,10},{10,11},{11... | collective-permute-start | bytes 24584 | tf_op jit(solution)/shard_map/ppermute | solution.py:17
  287.1 29.0 %collective-permute-start.11 = (f32[16,1,128]{2,1,0:T(1,128)S(1)}, f32[16,1,128]{2,1,0:T(1,128)S(1)}, u32[]{:S(2)}, u32[]{:S(2)}) collective-permute-start(f32[16,1,128]{2,1,0:T(1,128)S(1)} %get-tuple-element.84), channel_id=1, source_target_pairs={{1,0},{2,1},{3,2},{4,3},{5,4},{6,5},{7,6},{9,8},{10,9},{11,10},{12... | collective-permute-start | bytes 24584 | tf_op jit(solution)/shard_map/ppermute | solution.py:18
  316.2 5.5 %collective-permute-start.12 = (f32[16,18,1]{2,1,0:T(8,128)S(1)}, f32[16,18,1]{2,1,0:T(8,128)S(1)}, u32[]{:S(2)}, u32[]{:S(2)}) collective-permute-start(f32[16,18,1]{2,1,0:T(8,128)S(1)} %get-tuple-element.79), channel_id=1, source_target_pairs={{0,8},{8,16},{16,24},{1,9},{9,17},{17,25},{2,10},{10,18},{18,26},{... | collective-permute-start | bytes 3464 | tf_op jit(solution)/shard_map/ppermute | solution.py:17
  318.5 7.6 %collective-permute-start.13 = (f32[16,18,1]{2,1,0:T(8,128)S(1)}, f32[16,18,1]{2,1,0:T(8,128)S(1)}, u32[]{:S(2)}, u32[]{:S(2)}) collective-permute-start(f32[16,18,1]{2,1,0:T(8,128)S(1)} %get-tuple-element.80), channel_id=1, source_target_pairs={{8,0},{16,8},{24,16},{9,1},{17,9},{25,17},{10,2},{18,10},{26,18},{... | collective-permute-start | bytes 3464 | tf_op jit(solution)/shard_map/ppermute | solution.py:18
  361.0 4.4 %collective-permute-start.16 = (f32[8,1,256]{2,0,1:T(8,128)S(1)}, f32[8,1,256]{2,0,1:T(8,128)S(1)}, u32[]{:S(2)}, u32[]{:S(2)}) collective-permute-start(f32[8,1,256]{2,0,1:T(8,128)S(1)} %copy.223), channel_id=1, source_target_pairs={{1,0},{2,1},{3,2},{4,3},{5,4},{6,5},{7,6},{9,8},{10,9},{11,10},{12... | collective-permute-start | bytes 24584 | tf_op jit(solution)/shard_map/ppermute | solution.py:18
  363.0 5.9 %collective-permute-start.15 = (f32[8,1,256]{2,0,1:T(8,128)S(1)}, f32[8,1,256]{2,0,1:T(8,128)S(1)}, u32[]{:S(2)}, u32[]{:S(2)}) collective-permute-start(f32[8,1,256]{2,0,1:T(8,128)S(1)} %copy.221), channel_id=1, source_target_pairs={{0,1},{1,2},{2,3},{3,4},{4,5},{5,6},{6,7},{8,9},{9,10},{10,11},{11... | collective-permute-start | bytes 24584 | tf_op jit(solution)/shard_map/ppermute | solution.py:17
  369.1 4.4 %collective-permute-start.18 = (f32[8,1,256]{2,0,1:T(8,128)S(1)}, f32[8,1,256]{2,0,1:T(8,128)S(1)}, u32[]{:S(2)}, u32[]{:S(2)}) collective-permute-start(f32[8,1,256]{2,0,1:T(8,128)S(1)} %copy.230), channel_id=1, source_target_pairs={{1,0},{2,1},{3,2},{4,3},{5,4},{6,5},{7,6},{9,8},{10,9},{11,10},{12... | collective-permute-start | bytes 24584 | tf_op jit(solution)/shard_map/ppermute | solution.py:18
  371.0 5.9 %collective-permute-start.17 = (f32[8,1,256]{2,0,1:T(8,128)S(1)}, f32[8,1,256]{2,0,1:T(8,128)S(1)}, u32[]{:S(2)}, u32[]{:S(2)}) collective-permute-start(f32[8,1,256]{2,0,1:T(8,128)S(1)} %copy.228), channel_id=1, source_target_pairs={{0,1},{1,2},{2,3},{3,4},{4,5},{5,6},{6,7},{8,9},{9,10},{10,11},{11... | collective-permute-start | bytes 24584 | tf_op jit(solution)/shard_map/ppermute | solution.py:17
  (68 other events, 1071.1 us)
